TPU v7x, 256 devices: a whole 4x4x8 slice. The times are simulated.
256 devices in a mesh: blk: 64 (over z, x, core), rep: 4 (over y).
Axes of the slice: x: 4, y: 4, z: 8, core: 2. Of those that a mesh axis runs over, the one named last changes fastest.
Arguments:
- amplitudes: float32 [64, 64, 16, 512], P('blk', None, 'rep'), may hold values from -6 to 6
- cycle_integrals: float32 [32, 64, 64, 512], P('rep', None, 'blk'), may hold values from -0.09375 to 0.09375
- cross_integrals: float32 [32, 64, 64, 512], P('rep', None, 'blk'), may hold values from -0.09375 to 0.09375
- occ_energy: float32 [64], replicated, may hold values from -2 to -0.5
- vir_energy_a: float32 [32], replicated, may hold values from 0.2 to 3
- vir_energy_b: float32 [16], replicated, may hold values from 0.2 to 3
Outputs:
- update: float32 [64, 32, 16, 64], P('blk', 'rep')
- residual_rms: float32 [], replicated
All inputs are finite; a program needn't handle non-finite values.
Results may differ from a plain program's by a relative error of at most 0.0006.
Values sent between devices are 32-bit elements; how exact they have to be, the bound alone decides.
A program may use at most 64 MiB of HBM per device.

v0:
```python
import jax
import jax.numpy as jnp
from jax import lax
from jax.sharding import PartitionSpec as P


def per_device(
    amplitudes, cycle_integrals, cross_integrals, occ_energy, vir_energy_a, vir_energy_b
):
    highest = lax.Precision.HIGHEST
    whole = lax.all_gather(amplitudes, "rep", axis=2, tiled=True)
    moved = lax.all_to_all(whole, "blk", split_axis=1, concat_axis=0, tiled=True)
    crossed = jnp.swapaxes(moved, 0, 1)
    rows = amplitudes.shape[0]
    part = cycle_integrals
    cycle = lax.psum_scatter(
        jnp.einsum("aikc,kjbc->iabj", part, whole, precision=highest),
        "blk",
        scatter_dimension=0,
        tiled=True,
    )
    part = cross_integrals
    cross = lax.psum_scatter(
        jnp.einsum("aikc,kjbc->iabj", part, crossed, precision=highest),
        "blk",
        scatter_dimension=0,
        tiled=True,
    )
    residual = cycle + cross
    a_count = cycle_integrals.shape[0]
    occ_local = lax.dynamic_slice_in_dim(occ_energy, lax.axis_index("blk") * rows, rows, 0)
    vir_local = lax.dynamic_slice_in_dim(vir_energy_a, lax.axis_index("rep") * a_count, a_count, 0)
    denom = (
        occ_local[:, None, None, None]
        + occ_energy[None, None, None, :]
        - vir_local[None, :, None, None]
        - vir_energy_b[None, None, :, None]
    )
    update = residual / denom
    squares = lax.psum(jnp.sum(residual * residual), ("blk", "rep"))
    total_count = (
        occ_energy.shape[0] * occ_energy.shape[0] * vir_energy_a.shape[0] * vir_energy_b.shape[0]
    )
    residual_rms = jnp.sqrt(squares / total_count)
    return (update, residual_rms)


def solution(mesh):
    return jax.shard_map(
        per_device,
        mesh=mesh,
        in_specs=(
            P("blk", None, "rep", None),
            P("rep", None, "blk", None),
            P("rep", None, "blk", None),
            P(),
            P(),
            P(),
        ),
        out_specs=(P("blk", "rep", None, None), P()),
        check_vma=False,
    )
```

profile of v0, /device:TPU:1, one launch (start us, length us, event | category | flops | bytes accessed | tf_op | source)
XLA Modules:
  0.0 354.6 jit_solution(3494779001392865081)
XLA Ops:
  7.2 0.0 all-gather.2.cloned.1.call-start
  7.2 2.0 copy.9
  9.2 0.0 all-gather.2.cloned.1.call-update
  9.2 37.5 %all-gather.2.cloned.1.call-done = f32[1,64,16,512]{3,1,0,2:T(8,128)} async-done(((f32[1,64,4,512]{3,1,0,2:T(8,128)}), f32[1,64,16,512]{3,1,0,2:T(8,128)}) %all-gather.2.cloned.1.call-update) | async-done | bytes 2097168 | tf_op jit(solution)/shard_map/all_gather | solution.py:11
  46.8 4.2 %copy.11 = f32[1,64,16,512]{3,2,0,1:T(8,128)} copy(f32[1,64,16,512]{3,1,0,2:T(8,128)} %all-gather.2.cloned.1.call-done) | data formatting | bytes 4194304 | tf_op jit(solution)/shard_map/all_gather | solution.py:11
  50.9 0.0 copy-start
  50.9 0.0 copy-start.1
  50.9 11.3 %all-to-all-start = ((f32[1,64,16,512]{3,2,0,1:T(8,128)}), f32[1,64,16,512]{3,2,0,1:T(8,128)}, u32[]{:S(2)}, u32[]{:S(2)}) async-start(f32[1,64,16,512]{3,2,0,1:T(8,128)} %copy.11), calls=%async_computation | async-start | bytes 4194304 | tf_op jit(solution)/shard_map/all_to_all | solution.py:12
  62.2 0.0 reduce-scatter.4.cloned.1.call-start
  62.3 0.0 copy-done
  62.3 0.0 copy-done.1
  62.3 9.0 %fusion.1 = f32[64,16,8,64]{3,1,2,0:T(8,128)} fusion(f32[1,64,16,512]{3,1,0,2:T(8,128)S(1)} %copy-done, f32[8,64,1,512]{3,2,1,0:T(1,128)S(1)} %copy-done.1), kind=kOutput, calls=%fused_computation.2 | convolution fusion | flops 3221225472 | bytes 5242880 | tf_op jit(solution)/shard_map/aikc,kjbc->iabj/dot_general | solution.py:17
  71.3 40.6 %all-to-all-done = f32[1,64,16,512]{3,2,0,1:T(8,128)} async-done(((f32[1,64,16,512]{3,2,0,1:T(8,128)}), f32[1,64,16,512]{3,2,0,1:T(8,128)}, u32[]{:S(2)}, u32[]{:S(2)}) %all-to-all-start) | async-done | bytes 2097184 | tf_op jit(solution)/shard_map/all_to_all | solution.py:12
  111.9 10.5 %add_bitcast_fusion = f32[64,8,16,64]{0,2,1,3:T(8,128)} fusion(f32[64,16,8,64]{3,1,2,0:T(8,128)} %fusion.1, f32[1,64,16,512]{3,2,0,1:T(8,128)} %all-to-all-done, f32[8,64,1,512]{3,2,1,0:T(1,128)} %param.8), kind=kOutput, calls=%fused_computation | convolution fusion | flops 3221749760 | bytes 7340032 | tf_op jit(solution)/shard_map/aikc,kjbc->iabj/dot_general | solution.py:24
  122.4 6.1 %copy.12 = f32[64,8,16,64]{3,2,1,0:T(8,128)} copy(f32[64,8,16,64]{0,2,1,3:T(8,128)} %add_bitcast_fusion) | data formatting | bytes 4194304 | tf_op jit(solution)/shard_map/add | solution.py:29
  128.5 0.0 copy-start.4
  128.5 0.0 copy-start.3
  128.5 0.0 copy-start.2
  128.5 0.0 reduce-scatter.4.cloned.1.call-update
  128.5 0.6 copy-done.4
  129.1 0.6 dynamic_slice.6
  129.7 0.0 copy-done.3
  129.7 0.1 dynamic_slice.7
  129.8 0.6 broadcast_add_fusion
  130.4 0.1 broadcast_subtract_fusion
  130.5 133.6 %reduce-scatter.4.cloned.1.call-done = f32[1,8,16,64]{3,2,1,0:T(8,128)} async-done(((f32[64,8,16,64]{3,2,1,0:T(8,128)}), f32[1,8,16,64]{3,2,1,0:T(8,128)}) %reduce-scatter.4.cloned.1.call-update) | async-done | bytes 32784
  264.1 0.0 copy-done.2
  264.1 2.1 multiply_reduce_fusion
  266.2 79.7 %psum.7 = f32[]{:T(128)} all-reduce(f32[]{:T(128)} %get-tuple-element.4), channel_id=1, replica_groups=mesh['blk'=64,'rep'=4] {'blk','rep'}, use_global_device_ids=true, to_apply=%region_3.0 | all-reduce | flops 1 | bytes 8 | tf_op jit(solution)/shard_map/psum | solution.py:40
Async XLA Ops:
  7.2 39.6 %all-gather.2.cloned.1.call-start = ((), (), s32[]{:S(2)}) async-start(), calls=%async_computation.2 | async-start | bytes 2621440 | tf_op jit(solution)/shard_map/all_gather | solution.py:11
  50.9 11.3 %copy-start = (f32[1,64,16,512]{3,1,0,2:T(8,128)S(1)}, f32[1,64,16,512]{3,1,0,2:T(8,128)}, u32[]{:S(2)}) copy-start(f32[1,64,16,512]{3,1,0,2:T(8,128)} %all-gather.2.cloned.1.call-done) | copy-start | bytes 6291460
  50.9 11.3 %copy-start.1 = (f32[8,64,1,512]{3,2,1,0:T(1,128)S(1)}, f32[8,64,1,512]{3,2,1,0:T(1,128)}, u32[]{:S(2)}) copy-start(f32[8,64,1,512]{3,2,1,0:T(1,128)} %param.7) | copy-start | bytes 3145732
  50.9 60.9 %all-to-all-start = ((f32[1,64,16,512]{3,2,0,1:T(8,128)}), f32[1,64,16,512]{3,2,0,1:T(8,128)}, u32[]{:S(2)}, u32[]{:S(2)}) async-start(f32[1,64,16,512]{3,2,0,1:T(8,128)} %copy.11), calls=%async_computation | async-start | bytes 4194304 | tf_op jit(solution)/shard_map/all_to_all | solution.py:12
  62.2 201.9 %reduce-scatter.4.cloned.1.call-start = ((), (), s32[]{:S(2)}) async-start(), calls=%async_computation.3 | async-start | bytes 4259840
  128.5 0.7 copy-start.4
  128.5 1.2 copy-start.3
  128.5 135.6 %copy-start.2 = (f32[16]{0:T(128)S(1)}, f32[16]{0:T(128)}, u32[]{:S(2)}) copy-start(f32[16]{0:T(128)} %param.11) | copy-start | bytes 196
Sparse Core Ops, SparseCore 0:
  9.8 36.9 all-gather.1
  128.6 135.4 reduce-scatter.3
where the time goes:
time: 355 us
  waiting for transfers between devices  212 us (60%)
  blocking collectives  79.7 us (22%)
  matrix products  19.5 us (5%)
  between operations  15.9 us (4%)
  local copies, waits for them, and re-layouts  13.5 us (4%)
  starting transfers between devices  11.4 us (3%)
    unnamed x3, waiting for transfers between devices  134 us
    psum x1, blocking collectives, per_device(): squares = lax.psum(jnp.sum(residual * residual), ('blk', 'rep'))  79.7 us
    all_to_all x1, waiting for transfers between devices, per_device(): lax.all_to_all(whole, 'blk', split_axis=1, concat_axis=0, tiled=True)  40.6 us
    all_gather x1, waiting for transfers between devices, per_device(): whole = lax.all_gather(amplitudes, 'rep', axis=2, tiled=True)  37.5 us
    all_to_all x1, starting transfers between devices, per_device(): lax.all_to_all(whole, 'blk', split_axis=1, concat_axis=0, tiled=True)  11.3 us
    dot_general x1, matrix products, per_device(): jnp.einsum('aikc,kjbc->iabj', part, crossed, precision=highest)  10.5 us
    dot_general x1, matrix products, per_device(): jnp.einsum('aikc,kjbc->iabj', part, whole, precision=highest)  8.97 us
  transfers between devices with their start and end apart: 3, of which 3 were waited for; matrix products, arithmetic and copies ran while one was open for 3% of the time, Pallas kernels for 0%

commit v1 on v0

v1 whole, which is shorter than its diff:
```python
import functools

import jax
import jax.numpy as jnp
from jax import lax
from jax.experimental import pallas as pl
from jax.experimental.pallas import tpu as pltpu
from jax.sharding import PartitionSpec as P

MESH = pl.DeviceIdType.MESH
F32 = jnp.float32
BF16 = jnp.bfloat16
NY = 4
NB = 4
NA = 8
NC = 512
CT = NC // 128
ROWS = NB * CT
KT = 3 * NC


def ring_order(n):
    order = [0]
    for d in range(1, n // 2 + 1):
        order.append(d)
        if n - d != d:
            order.append(n - d)
    return order


def kernel(
    nz, nx,
    t_hbm, w_hbm, x_hbm, res_ref, rms_ref,
    tb, tt, a1, wv, xv, wop, top, part, ra, s1, rb, s2, rc, ssz, ssx, ssy,
    load_sem, ty_send, ty_recv, tf_send, tf_recv, z_send, z_recv, c_send, c_recv, c_loc,
    tty_send, tty_recv, ttf_send, ttf_recv, ra_send, ra_recv, rb_send, rb_recv, rc_send, rc_recv,
    ss_send, ss_recv,
):
    nxc = nx * 2
    no = nz * nxc
    blk_rows = no * ROWS
    me, y = lax.axis_index("blk"), lax.axis_index("rep")
    z, xc = me // nxc, me % nxc
    x, core = xc // 2, xc % 2
    up, down, far = (y + 1) % NY, (y + NY - 1) % NY, (y + 2) % NY
    order = ring_order(nz)

    def at_y(yy):
        return {"blk": me, "rep": yy}

    def at_blk(b):
        return {"blk": b, "rep": y}

    def zpeer(d):
        return (z + d) % nz

    def xcpeer(d):
        return (xc + d) % nxc

    def send(src, dst, ssem, rsem, dev):
        pltpu.make_async_remote_copy(
            src_ref=src, dst_ref=dst, send_sem=ssem, recv_sem=rsem, device_id=dev, device_id_type=MESH
        ).start()

    def arrived(ref, sem):
        pltpu.make_async_copy(ref, ref, sem).wait()

    def rows(start, n):
        return pl.ds(pl.multiple_of(start, ROWS), n)

    barrier = pltpu.get_barrier_semaphore()
    count = 0
    for d in range(1, nz):
        pl.semaphore_signal(barrier, inc=1, device_id=at_blk(zpeer(d) * nxc + xc), device_id_type=MESH)
        count += 1
    for d in range(1, nxc):
        pl.semaphore_signal(barrier, inc=1, device_id=at_blk(z * nxc + xcpeer(d)), device_id_type=MESH)
        count += 1
    for yy in (up, down, far):
        pl.semaphore_signal(barrier, inc=1, device_id=at_y(yy), device_id_type=MESH)
        count += 1
    pl.semaphore_wait(barrier, count)

    half = blk_rows // 2
    mine = y * blk_rows

    for h in (0, 1):
        send(t_hbm.at[rows(h * half, half)], tb.at[rows(mine + h * half, half)],
             ty_send, ty_recv.at[0, h], at_y(up))
        g = 1 - h
        send(t_hbm.at[rows(g * half, half)], tb.at[rows(mine + g * half, half)],
             ty_send, ty_recv.at[1, g], at_y(down))

    zrows = nxc * ROWS
    for d in order[1:]:
        zp = zpeer(d)
        send(t_hbm.at[rows(zp * zrows, zrows)], a1.at[rows(z * zrows, zrows)],
             z_send, z_recv.at[z], at_blk(zp * nxc + xc))

    def second_stage(src, zs):
        for d in range(1, nxc):
            p = xcpeer(d)
            send(src.at[rows(zs * zrows + p * ROWS, ROWS)], tt.at[rows(mine + zs * zrows + xc * ROWS, ROWS)],
                 c_send, c_recv.at[zs], at_blk(z * nxc + p))
        pltpu.make_async_copy(
            src.at[rows(zs * zrows + xc * ROWS, ROWS)], tt.at[rows(mine + zs * zrows + xc * ROWS, ROWS)],
            c_loc.at[zs]).start()

    second_stage(t_hbm, z)
    load_w = pltpu.make_async_copy(w_hbm, wv.at[pl.ds(0, NA * no * CT)], load_sem.at[0])
    load_x = pltpu.make_async_copy(x_hbm, xv.at[pl.ds(0, NA * no * CT)], load_sem.at[1])
    load_t = pltpu.make_async_copy(t_hbm, tb.at[rows(mine, blk_rows)], load_sem.at[2])
    load_w.start()
    load_x.start()
    load_t.start()

    def split(v):
        hi = v.astype(BF16)
        return hi, (v - hi.astype(F32)).astype(BF16)

    def prep_integrals(src, term):
        stride = no * CT

        def step(i2, carry):
            out = pl.ds(pl.multiple_of(i2 * 16, 16), 16)
            for ct in range(CT):
                v = jnp.concatenate(
                    [src[pl.ds((i2 * 2 + e) * CT + ct, NA, stride=stride), :] for e in range(2)], axis=0)
                hi, lo = split(v)
                base = term * KT + ct * 128
                wop[out, base:base + 128] = hi
                wop[out, base + NC:base + NC + 128] = lo
                wop[out, base + 2 * NC:base + 2 * NC + 128] = hi
            return carry

        lax.fori_loop(0, no // 2, step, 0)

    def prep_amplitudes(src, yb, term):
        def step(b, carry):
            out = pl.ds(pl.multiple_of(b * no, no), no)
            for ct in range(CT):
                v = src[pl.ds(yb * blk_rows + ct * NB + b, no, stride=ROWS), :]
                hi, lo = split(v)
                base = term * KT + ct * 128
                top[out, base:base + 128] = hi
                top[out, base + NC:base + NC + 128] = hi
                top[out, base + 2 * NC:base + 2 * NC + 128] = lo
            return carry

        lax.fori_loop(0, NB, step, 0)

    def multiply(slot, term):
        def step(kk, carry):
            cols = pl.ds(pl.multiple_of(term * KT + kk * NC, NC), NC)
            p = lax.dot_general(
                wop[:, cols], top[:, cols], (((1,), (1,)), ((), ())), preferred_element_type=F32)
            part[slot] += p.reshape(nz * nx, 2, NA, NB * no)
            return carry

        lax.fori_loop(0, KT // NC, step, 0)

    def cycle_term(slot, yb):
        part[slot] = jnp.zeros(part.shape[1:], F32)
        prep_amplitudes(tb, yb, 0)
        multiply(slot, 0)

    def cross_term(slot, yb):
        prep_amplitudes(tt, yb, 1)
        multiply(slot, 1)

    def core_stage(slot):
        send(part.at[slot, :, 1 - core], ra.at[slot], ra_send, ra_recv.at[slot], at_blk(z * nxc + x * 2 + 1 - core))

    def x_stage(slot):
        arrived(ra.at[slot], ra_recv.at[slot])
        s1[slot] = (part[slot, :, core] + ra[slot]).reshape(nz, nx, NA, NB * no)
        for d in range(1, nx):
            p = (x + d) % nx
            send(s1.at[slot, :, p], rb.at[slot, d - 1], rb_send, rb_recv.at[slot], at_blk(z * nxc + p * 2 + core))

    def z_stage(slot):
        arrived(rb.at[slot], rb_recv.at[slot])
        total = s1[slot, :, x]
        for d in range(nx - 1):
            total = total + rb[slot, d]
        s2[slot] = total
        for d in range(1, nz):
            p = zpeer(d)
            send(s2.at[slot, p], rc.at[slot, d - 1], rc_send, rc_recv.at[slot], at_blk(p * nxc + xc))

    def final(slot, yb):
        arrived(rc.at[slot], rc_recv.at[slot])
        total = s2[slot, z]
        for d in range(nz - 1):
            total = total + rc[slot, d]
        res_ref[:, pl.ds(pl.multiple_of(yb * NB * no, NB * no), NB * no)] = total
        sq = total * total
        if NB * no < 128:
            sq = jnp.concatenate([sq, jnp.zeros((NA, 128 - NB * no), F32)], axis=1)
        out = sq[:, 0:128]
        for n in range(1, NB * no // 128):
            out = out + sq[:, n * 128:(n + 1) * 128]
        return out

    def relay_stage(d):
        zs = (z + d) % nz
        arrived(a1.at[rows(zs * zrows, zrows)], z_recv.at[zs])
        second_stage(a1, zs)

    load_w.wait()
    prep_integrals(wv, 0)
    for d in order[1:3]:
        relay_stage(d)
    first = tb.at[rows(down * blk_rows, half)]
    arrived(first, ty_recv.at[0, 0])
    send(first, first, tf_send, tf_recv.at[0], at_y(up))
    second = tb.at[rows(up * blk_rows + half, half)]
    arrived(second, ty_recv.at[1, 1])
    send(second, second, tf_send, tf_recv.at[1], at_y(down))
    load_x.wait()
    prep_integrals(xv, 1)
    for d in order[3:]:
        relay_stage(d)

    for q, d in enumerate(order):
        zs = (z + d) % nz
        arrived(tt.at[rows(mine + zs * zrows, zrows - ROWS)], c_recv.at[zs])
        arrived(tt.at[rows(mine + zs * zrows, ROWS)], c_loc.at[zs])
        chunk = tt.at[rows(mine + zs * zrows, zrows)]
        send(chunk, chunk, tty_send, tty_recv.at[0, q], at_y(up))
        send(chunk, chunk, tty_send, tty_recv.at[1, q], at_y(down))

    load_t.wait()
    cycle_term(0, y)
    cross_term(0, y)
    core_stage(0)

    def forward(q):
        zs = (z + order[q]) % nz
        way = q % 2
        src_y, dst_y = ((down, up), (up, down))[way]
        chunk = tt.at[rows(src_y * blk_rows + zs * zrows, zrows)]
        arrived(chunk, tty_recv.at[way, q])
        send(chunk, chunk, ttf_send, ttf_recv.at[q], at_y(dst_y))

    for q in range(nz // 2):
        forward(q)
    arrived(tb.at[rows(down * blk_rows + half, half)], ty_recv.at[0, 1])
    cycle_term(1, down)
    x_stage(0)
    for q in range(nz // 2, nz):
        forward(q)
    for q, d in enumerate(order):
        if q % 2 == 1:
            zs = (z + d) % nz
            arrived(tt.at[rows(down * blk_rows + zs * zrows, zrows)], tty_recv.at[0, q])
    cross_term(1, down)
    core_stage(1)
    z_stage(0)
    arrived(tb.at[rows(up * blk_rows, half)], ty_recv.at[1, 0])
    cycle_term(2, up)
    for q, d in enumerate(order):
        if q % 2 == 0:
            zs = (z + d) % nz
            arrived(tt.at[rows(up * blk_rows + zs * zrows, zrows)], tty_recv.at[1, q])
    cross_term(2, up)
    core_stage(2)
    x_stage(1)
    arrived(tb.at[rows(far * blk_rows, half)], tf_recv.at[0])
    arrived(tb.at[rows(far * blk_rows + half, half)], tf_recv.at[1])
    cycle_term(3, far)
    x_stage(2)
    ss = final(0, y)
    for q, d in enumerate(order):
        zs = (z + d) % nz
        arrived(tt.at[rows(far * blk_rows + zs * zrows, zrows)], ttf_recv.at[q])
    cross_term(3, far)
    core_stage(3)
    z_stage(1)
    z_stage(2)
    x_stage(3)
    ss = ss + final(1, down)
    ss = ss + final(2, up)
    z_stage(3)
    ss = ss + final(3, far)

    def add_slots(ref, n):
        total = ref[0]
        for k in range(1, n):
            total = total + ref[k]
        return total

    ssz[z] = ss
    for d in range(1, nz):
        send(ssz.at[z], ssz.at[z], ss_send.at[0], ss_recv.at[0], at_blk(zpeer(d) * nxc + xc))
    arrived(ssz.at[pl.ds(0, nz - 1)], ss_recv.at[0])
    ssx[xc] = add_slots(ssz, nz)
    for d in range(1, nxc):
        send(ssx.at[xc], ssx.at[xc], ss_send.at[1], ss_recv.at[1], at_blk(z * nxc + xcpeer(d)))
    arrived(ssx.at[pl.ds(0, nxc - 1)], ss_recv.at[1])
    ssy[y] = add_slots(ssx, nxc)
    for yy in (up, down, far):
        send(ssy.at[y], ssy.at[y], ss_send.at[2], ss_recv.at[2], at_y(yy))
    arrived(ssy.at[pl.ds(0, NY - 1)], ss_recv.at[2])
    total = jnp.sum(add_slots(ssy, NY), keepdims=True)
    size = no * no * NA * NY * NB * NY
    rms_ref[...] = jnp.broadcast_to(jnp.sqrt(total / size), rms_ref.shape)

    arrived(tb.at[rows(0, 2 * blk_rows)], ty_send)
    arrived(tb.at[rows(0, blk_rows)], tf_send)
    arrived(a1.at[rows(0, (nz - 1) * zrows)], z_send)
    arrived(tt.at[rows(0, nz * (nxc - 1) * ROWS)], c_send)
    arrived(tt.at[rows(0, 2 * blk_rows)], tty_send)
    arrived(tt.at[rows(0, blk_rows)], ttf_send)
    arrived(ra, ra_send)
    if nx > 1:
        arrived(rb, rb_send)
    arrived(rc, rc_send)
    arrived(ssz.at[pl.ds(0, nz - 1)], ss_send.at[0])
    arrived(ssx.at[pl.ds(0, nxc - 1)], ss_send.at[1])
    arrived(ssy.at[pl.ds(0, NY - 1)], ss_send.at[2])


def residual_parts(nz, nx, t, w, x):
    nxc = nx * 2
    no = nz * nxc
    n = NB * no
    dma = pltpu.SemaphoreType.DMA
    return pl.pallas_call(
        functools.partial(kernel, nz, nx),
        out_shape=(jax.ShapeDtypeStruct((NA, NY * n), F32), jax.ShapeDtypeStruct((8, 128), F32)),
        in_specs=[pl.BlockSpec(memory_space=pl.ANY)] * 3,
        out_specs=(pl.BlockSpec(memory_space=pltpu.VMEM), pl.BlockSpec(memory_space=pltpu.VMEM)),
        scratch_shapes=[
            pltpu.VMEM((NY * no * ROWS + ROWS, 128), F32),
            pltpu.VMEM((NY * no * ROWS + ROWS, 128), F32),
            pltpu.VMEM((no * ROWS, 128), F32),
            pltpu.VMEM(((NA + 1) * no * CT, 128), F32),
            pltpu.VMEM(((NA + 1) * no * CT, 128), F32),
            pltpu.VMEM((NA * no, 2 * KT), BF16),
            pltpu.VMEM((n, 2 * KT), BF16),
            pltpu.VMEM((NY, nz * nx, 2, NA, n), F32),
            pltpu.VMEM((NY, nz * nx, NA, n), F32),
            pltpu.VMEM((NY, nz, nx, NA, n), F32),
            pltpu.VMEM((NY, max(nx - 1, 1), nz, NA, n), F32),
            pltpu.VMEM((NY, nz, NA, n), F32),
            pltpu.VMEM((NY, nz - 1, NA, n), F32),
            pltpu.VMEM((nz, 8, 128), F32),
            pltpu.VMEM((nxc, 8, 128), F32),
            pltpu.VMEM((NY, 8, 128), F32),
            dma((3,)),
            dma, dma((2, 2)), dma, dma((2,)),
            dma, dma((nz,)), dma, dma((nz,)), dma((nz,)),
            dma, dma((2, nz)), dma, dma((nz,)),
            dma, dma((NY,)), dma, dma((NY,)), dma, dma((NY,)),
            dma((3,)), dma((3,)),
        ],
        compiler_params=pltpu.CompilerParams(collective_id=0, has_side_effects=True),
    )(t, w, x)


def per_device(nz, nx, amplitudes, cycle_integrals, cross_integrals, occ_energy, vir_energy_a, vir_energy_b):
    no = nz * nx * 2
    t = amplitudes.reshape(no, NB, CT, 128).transpose(0, 2, 1, 3).reshape(no * ROWS, 128)
    w = cycle_integrals.reshape(NA * no * CT, 128)
    x = cross_integrals.reshape(NA * no * CT, 128)
    res, rms = residual_parts(nz, nx, t, w, x)
    residual = res.reshape(1, NA, NB * NY, no)
    occ_local = lax.dynamic_slice_in_dim(occ_energy, lax.axis_index("blk"), 1, 0)
    vir_local = lax.dynamic_slice_in_dim(vir_energy_a, lax.axis_index("rep") * NA, NA, 0)
    denom = (
        occ_local[:, None, None, None]
        + occ_energy[None, None, None, :]
        - vir_local[None, :, None, None]
        - vir_energy_b[None, None, :, None]
    )
    return residual / denom, rms[0, 0]


def solution(mesh, nz=8, nx=4):
    return jax.shard_map(
        functools.partial(per_device, nz, nx),
        mesh=mesh,
        in_specs=(
            P("blk", None, "rep", None),
            P("rep", None, "blk", None),
            P("rep", None, "blk", None),
            P(),
            P(),
            P(),
        ),
        out_specs=(P("blk", "rep", None, None), P()),
        check_vma=False,
    )
```

time: 355 us -> 83 us (0.23)
  waiting for transfers between devices: 212 us -> 0 us
  blocking collectives: 79.7 us -> 0 us
  Pallas kernels: 0 us -> 76.1 us
  matrix products: 19.5 us -> 0 us
  between operations: 15.9 us -> 0.66 us
  starting transfers between devices: 11.4 us -> 0 us
  local copies, waits for them, and re-layouts: 13.5 us -> 4.57 us
    unnamed x3 -> x0, waiting for transfers between devices: 134 us -> none
    psum x1 -> x0, blocking collectives: 79.7 us -> none  [per_device(): squares = lax.psum(jnp.sum(residual * residual), ('blk', 'rep'))]
    pallas_call x0 -> x1, Pallas kernels: none -> 76.1 us  [residual_parts(): pl.pallas_call(functools.partial(kernel, nz, nx), out_shape=(jax.ShapeDty...]
    all_to_all x1 -> x0, waiting for transfers between devices: 40.6 us -> none  [per_device(): lax.all_to_all(whole, 'blk', split_axis=1, concat_axis=0, tiled=True)]
    all_gather x1 -> x0, waiting for transfers between devices: 37.5 us -> none  [per_device(): whole = lax.all_gather(amplitudes, 'rep', axis=2, tiled=True)]
    dot_general x2 -> x0, matrix products: 19.5 us -> none  [the longest x1 10.5 us: per_device(): jnp.einsum('aikc,kjbc->iabj', part, crossed, precision=highest)]
    all_to_all x1 -> x0, starting transfers between devices: 11.3 us -> none  [per_device(): lax.all_to_all(whole, 'blk', split_axis=1, concat_axis=0, tiled=True)]
    add x1 -> x0, local copies, waits for them, and re-layouts: 6.07 us -> none  [per_device(): residual = cycle + cross]
  transfers between devices with their start and end apart: 3 -> 0, of which waited for: 3 -> 0; matrix products, arithmetic and copies ran while one was open for 3% -> 0% of each run, Pallas kernels for 0% -> 0%
where the time goes in v1:
time: 83 us; the launch traced here: 82.8 us
  Pallas kernels  76.1 us (92%)
  local copies, waits for them, and re-layouts  4.57 us (6%)
  other arithmetic  1.43 us (2%)
    pallas_call x1, Pallas kernels, residual_parts(): pl.pallas_call(functools.partial(kernel, nz, nx), out_shape=(jax.ShapeDty...  76.1 us
    unnamed x6, local copies, waits for them, and re-layouts  1.89 us

profile of v1, /device:TPU:1, one launch (start us, length us, event | category | flops | bytes accessed | tf_op | source)
XLA Modules:
  0.0 82.8 jit_solution(14662195476677580358)
XLA Ops:
  0.6 76.1 %shard_map.77 = (f32[8,1024]{1,0:T(8,128)}, f32[8,128]{1,0:T(8,128)}) custom-call(f32[1024,128]{1,0:T(8,128)} %bitcast.11, f32[2048,128]{1,0:T(8,128)} %bitcast.9, f32[2048,128]{1,0:T(8,128)} %bitcast.10), custom_call_target="tpu_custom_call" | custom-call | tf_op jit(solution)/shard_map/pallas_call | solution.py:329
  76.7 0.8 %reshape.79 = f32[1,8,16,64]{3,2,1,0:T(8,128)S(1)} reshape(f32[8,1024]{1,0:T(8,128)} %get-tuple-element.4) | data formatting | bytes 65536 | tf_op jit(solution)/shard_map/reshape | solution.py:368
  77.6 0.0 copy-start.1
  77.6 0.7 copy-done.1
  78.2 0.1 dynamic_slice.7
  78.3 0.0 copy-start.2
  78.3 0.7 copy-done.2
  79.0 0.6 dynamic_slice.6
  79.5 0.6 broadcast_add_fusion
  80.2 0.0 copy-start
  80.2 0.1 broadcast_subtract_fusion
  80.3 0.6 copy-done
  80.8 0.7 subtract_divide_fusion
  81.6 1.2 %slice.3 = f32[1,1]{1,0:T(1,128)} slice(f32[8,128]{1,0:T(8,128)} %get-tuple-element.5), slice={[0:1], [0:1]} | slice | bytes 8 | tf_op jit(solution)/shard_map/slice | solution.py:377
Async XLA Ops:
  77.6 0.7 copy-start.1
  78.3 0.7 copy-start.2
  80.2 0.7 copy-start

commit v2 on v1

v2 whole, which is shorter than its diff:
```python
import functools

import jax
import jax.numpy as jnp
from jax import lax
from jax.experimental import pallas as pl
from jax.experimental.pallas import tpu as pltpu
from jax.sharding import PartitionSpec as P

MESH = pl.DeviceIdType.MESH
F32 = jnp.float32
BF16 = jnp.bfloat16
NY = 4
NB = 4
NA = 8
NC = 512
CT = NC // 128
ROWS = NB * CT
KT = 3 * NC


def ring_order(n):
    order = [0]
    for d in range(1, n // 2 + 1):
        order.append(d)
        if n - d != d:
            order.append(n - d)
    return order


def kernel(
    nz, nx,
    t_hbm, w_hbm, x_hbm, occ_hbm, va_hbm, vb_hbm, upd_ref, rms_ref,
    tb, tt, a1, wv, xv, occ_v, va_v, vb_v, den, wop, top, part, ra, s1, rx, rb, rd, s2, rc, ssz, ssp,
    load_sem, ty_send, ty_recv, tf_send, tf_recv, z_send, z_recv, c_send, c_recv, c_loc,
    tty_send, tty_recv, ttf_send, ttf_recv, ra_send, ra_recv, rx_send, rx_recv, rb_send, rb_recv, rd_send, rd_recv, rc_send, rc_recv,
    ss_send, ss_recv,
):
    nxc = nx * 2
    no = nz * nxc
    blk_rows = no * ROWS
    hj = no // 2
    pc = NB * hj
    me, y = lax.axis_index("blk"), lax.axis_index("rep")
    z, xc = me // nxc, me % nxc
    x, core = xc // 2, xc % 2
    up, down, far = (y + 1) % NY, (y + NY - 1) % NY, (y + 2) % NY
    right, left, across = (x + 1) % nx, (x + nx - 1) % nx, (x + 2) % nx
    slot_y = (y, down, up, far)
    order = ring_order(nz)

    def at_y(yy):
        return {"blk": me, "rep": yy}

    def at_blk(b):
        return {"blk": b, "rep": y}

    def zpeer(d):
        return (z + d) % nz

    def xcpeer(d):
        return (xc + d) % nxc

    def send(src, dst, ssem, rsem, dev):
        pltpu.make_async_remote_copy(
            src_ref=src, dst_ref=dst, send_sem=ssem, recv_sem=rsem, device_id=dev, device_id_type=MESH
        ).start()

    def arrived(ref, sem):
        pltpu.make_async_copy(ref, ref, sem).wait()

    def rows(start, n):
        return pl.ds(pl.multiple_of(start, ROWS), n)

    barrier = pltpu.get_barrier_semaphore()
    count = 0
    for d in range(1, nz):
        pl.semaphore_signal(barrier, inc=1, device_id=at_blk(zpeer(d) * nxc + xc), device_id_type=MESH)
        count += 1

    def plane_peers():
        for e in (1, NY - 1, 0, 2):
            for d in range(nxc):
                if d or e:
                    yield {"blk": z * nxc + xcpeer(d), "rep": (y + e) % NY}

    for peer in plane_peers():
        pl.semaphore_signal(barrier, inc=1, device_id=peer, device_id_type=MESH)
        count += 1
    pl.semaphore_wait(barrier, count)

    half = blk_rows // 2
    mine = y * blk_rows

    for h in (0, 1):
        send(t_hbm.at[rows(h * half, half)], tb.at[rows(mine + h * half, half)],
             ty_send, ty_recv.at[0, h], at_y(up))
        g = 1 - h
        send(t_hbm.at[rows(g * half, half)], tb.at[rows(mine + g * half, half)],
             ty_send, ty_recv.at[1, g], at_y(down))

    zrows = nxc * ROWS
    for d in order[1:]:
        zp = zpeer(d)
        send(t_hbm.at[rows(zp * zrows, zrows)], a1.at[rows(z * zrows, zrows)],
             z_send, z_recv.at[z], at_blk(zp * nxc + xc))

    def second_stage(src, zs):
        for d in range(1, nxc):
            p = xcpeer(d)
            send(src.at[rows(zs * zrows + p * ROWS, ROWS)], tt.at[rows(mine + zs * zrows + xc * ROWS, ROWS)],
                 c_send, c_recv.at[zs], at_blk(z * nxc + p))
        pltpu.make_async_copy(
            src.at[rows(zs * zrows + xc * ROWS, ROWS)], tt.at[rows(mine + zs * zrows + xc * ROWS, ROWS)],
            c_loc.at[zs]).start()

    second_stage(t_hbm, z)
    load_w = pltpu.make_async_copy(w_hbm, wv.at[pl.ds(0, NA * no * CT)], load_sem.at[0])
    load_x = pltpu.make_async_copy(x_hbm, xv.at[pl.ds(0, NA * no * CT)], load_sem.at[1])
    load_t = pltpu.make_async_copy(t_hbm, tb.at[rows(mine, blk_rows)], load_sem.at[2])
    load_w.start()
    load_x.start()
    load_t.start()
    load_e = [
        pltpu.make_async_copy(src, dst, load_sem.at[3 + k])
        for k, (src, dst) in enumerate(((occ_hbm, occ_v), (va_hbm, va_v), (vb_hbm, vb_v)))
    ]
    for copy in load_e:
        copy.start()

    def split(v):
        hi = v.astype(BF16)
        return hi, (v - hi.astype(F32)).astype(BF16)

    def prep_integrals(src, term):
        stride = no * CT

        def step(i2, carry):
            out = pl.ds(pl.multiple_of(i2 * 16, 16), 16)
            for ct in range(CT):
                v = jnp.concatenate(
                    [src[pl.ds((i2 * 2 + e) * CT + ct, NA, stride=stride), :] for e in range(2)], axis=0)
                hi, lo = split(v)
                base = term * KT + ct * 128
                wop[out, base:base + 128] = hi
                wop[out, base + NC:base + NC + 128] = lo
                wop[out, base + 2 * NC:base + 2 * NC + 128] = hi
            return carry

        lax.fori_loop(0, no // 2, step, 0)

    def prep_amplitudes(src, yb, term, h):
        def step(b, carry):
            out = pl.ds(pl.multiple_of(h * pc + b * hj, hj), hj)
            for ct in range(CT):
                v = src[pl.ds(yb * blk_rows + h * hj * ROWS + ct * NB + b, hj, stride=ROWS), :]
                hi, lo = split(v)
                base = term * KT + ct * 128
                top[out, base:base + 128] = hi
                top[out, base + NC:base + NC + 128] = hi
                top[out, base + 2 * NC:base + 2 * NC + 128] = lo
            return carry

        lax.fori_loop(0, NB, step, 0)

    def product(term, kk, r):
        cols = pl.ds(pl.multiple_of(term * KT + kk * NC, NC), NC)
        p = lax.dot_general(wop[:, cols], top[r, cols], (((1,), (1,)), ((), ())), preferred_element_type=F32)
        return p.reshape(nz * nx, 2, NA, p.shape[1])

    def cycle_term(slot):
        for h in (0, 1):
            prep_amplitudes(tb, slot_y[slot], 0, h)
        part[slot] = product(0, 0, slice(None))

        def step(kk, carry):
            part[slot] += product(0, kk, slice(None))
            return carry

        lax.fori_loop(1, KT // NC, step, 0)

    def cross_term(slot, h):
        prep_amplitudes(tt, slot_y[slot], 1, h)
        c = slice(h * pc, (h + 1) * pc)

        def step(kk, carry):
            part[slot, :, :, :, c] += product(1, kk, c)
            return carry

        lax.fori_loop(0, KT // NC, step, 0)

    def core_stage(slot, h):
        c = slice(h * pc, (h + 1) * pc)
        n = slot * 2 + h
        send(part.at[slot, :, 1 - core, :, c], ra.at[n], ra_send, ra_recv.at[n], at_blk(z * nxc + x * 2 + 1 - core))

    hz = nz // 2

    def x_stage1(slot, h):
        c = slice(h * pc, (h + 1) * pc)
        n = slot * 2 + h
        arrived(ra.at[n], ra_recv.at[n])
        s1[n] = (part[slot, :, core, :, c] + ra[n]).reshape(nz, nx, NA, pc)
        send(s1.at[n, 0:hz, across], rx.at[n, 0], rx_send, rx_recv.at[n, 0], at_blk(z * nxc + right * 2 + core))
        send(s1.at[n, hz:nz, across], rx.at[n, 1], rx_send, rx_recv.at[n, 1], at_blk(z * nxc + left * 2 + core))

    def x_stage2(slot, h):
        n = slot * 2 + h
        arrived(rx.at[n, 0], rx_recv.at[n, 0])
        s1[n, 0:hz, right] += rx[n, 0]
        send(s1.at[n, :, right], rb.at[n, 0], rb_send, rb_recv.at[n, 0], at_blk(z * nxc + right * 2 + core))
        arrived(rx.at[n, 1], rx_recv.at[n, 1])
        s1[n, hz:nz, left] += rx[n, 1]
        send(s1.at[n, :, left], rb.at[n, 1], rb_send, rb_recv.at[n, 1], at_blk(z * nxc + left * 2 + core))

    def x_direct(h):
        c = slice(h * pc, (h + 1) * pc)
        n = 6 + h
        arrived(ra.at[n], ra_recv.at[n])
        s1[n] = (part[3, :, core, :, c] + ra[n]).reshape(nz, nx, NA, pc)
        for d in (2, 1, 3):
            p = (x + d) % nx
            send(s1.at[n, :, p], rd.at[h, d - 1], rd_send, rd_recv.at[h], at_blk(z * nxc + p * 2 + core))

    def z_stage(slot, h):
        n = slot * 2 + h
        if slot == 3:
            arrived(rd.at[h], rd_recv.at[h])
            s2[n] = s1[n, :, x] + rd[h, 0] + rd[h, 1] + rd[h, 2]
        else:
            for k in (0, 1):
                arrived(rb.at[n, k], rb_recv.at[n, k])
            s2[n] = s1[n, :, x] + rb[n, 0] + rb[n, 1]
        for d in order[::-1][:-1]:
            p = zpeer(d)
            send(s2.at[n, p], rc.at[n, d - 1], rc_send, rc_recv.at[n], at_blk(p * nxc + xc))

    def final(slot, h):
        n = slot * 2 + h
        arrived(rc.at[n], rc_recv.at[n])
        total = s2[n, z]
        for d in range(nz - 1):
            total = total + rc[n, d]
        up_date = total / den[n]
        for b in range(NB):
            upd_ref[slot_y[slot] * NB + b, :, h * hj:(h + 1) * hj] = up_date[:, b * hj:(b + 1) * hj]
        sq = jnp.sum(total * total, axis=0, keepdims=True)
        if pc < 128:
            sq = jnp.concatenate([sq, jnp.zeros((1, 128 - pc), F32)], axis=1)
        return sq

    def denominators():
        for copy in load_e:
            copy.wait()

        def pick(ref, at):
            lane = lax.broadcasted_iota(jnp.int32, ref.shape, 1)
            return jnp.sum(jnp.where(lane == at, ref[...], 0.0), axis=1, keepdims=True)

        mine_o = pick(occ_v, me)
        wide = (NA, va_v.shape[1])
        lane = lax.broadcasted_iota(jnp.int32, wide, 1)
        sub = lax.broadcasted_iota(jnp.int32, wide, 0)
        va = jnp.sum(
            jnp.where(lane == y * NA + sub, jnp.broadcast_to(va_v[...], wide), 0.0), axis=1, keepdims=True)
        for h in (0, 1):
            occ = jnp.concatenate([occ_v[:, h * hj:(h + 1) * hj]] * NB, axis=1)
            for slot in range(NY):
                vb = jnp.concatenate(
                    [jnp.broadcast_to(pick(vb_v, slot_y[slot] * NB + b), (1, hj)) for b in range(NB)], axis=1)
                den[slot * 2 + h] = ((mine_o + occ) - va) - vb

    def relay_stage(d):
        zs = (z + d) % nz
        arrived(a1.at[rows(zs * zrows, zrows)], z_recv.at[zs])
        second_stage(a1, zs)

    load_w.wait()
    prep_integrals(wv, 0)
    for d in order[1:3]:
        relay_stage(d)
    first = tb.at[rows(down * blk_rows, half)]
    arrived(first, ty_recv.at[0, 0])
    send(first, first, tf_send, tf_recv.at[0], at_y(up))
    second = tb.at[rows(up * blk_rows + half, half)]
    arrived(second, ty_recv.at[1, 1])
    send(second, second, tf_send, tf_recv.at[1], at_y(down))
    load_x.wait()
    prep_integrals(xv, 1)
    for d in order[3:]:
        relay_stage(d)
    denominators()
    load_t.wait()
    cycle_term(0)

    for q in range(nz):
        arrived(tt.at[rows(mine + q * zrows, zrows - ROWS)], c_recv.at[q])
        arrived(tt.at[rows(mine + q * zrows, ROWS)], c_loc.at[q])
        chunk = tt.at[rows(mine + q * zrows, zrows)]
        send(chunk, chunk, tty_send, tty_recv.at[0, q], at_y(up))
        send(chunk, chunk, tty_send, tty_recv.at[1, q], at_y(down))

    cross_term(0, 0)
    core_stage(0, 0)
    cross_term(0, 1)
    core_stage(0, 1)
    arrived(tb.at[rows(down * blk_rows + half, half)], ty_recv.at[0, 1])
    cycle_term(1)
    x_stage1(0, 0)
    x_stage1(0, 1)
    arrived(tb.at[rows(up * blk_rows, half)], ty_recv.at[1, 0])
    cycle_term(2)
    x_stage2(0, 0)
    x_stage2(0, 1)
    arrived(tb.at[rows(far * blk_rows, half)], tf_recv.at[0])
    arrived(tb.at[rows(far * blk_rows + half, half)], tf_recv.at[1])
    cycle_term(3)
    z_stage(0, 0)
    z_stage(0, 1)

    def near(h):
        for q in range(h * hz, (h + 1) * hz):
            for way, src_y in enumerate((down, up)):
                chunk = tt.at[rows(src_y * blk_rows + q * zrows, zrows)]
                arrived(chunk, tty_recv.at[way, q])
                if q % 2 == way:
                    send(chunk, chunk, ttf_send, ttf_recv.at[q], at_y((up, down)[way]))

    def distant(h):
        for q in range(h * hz, (h + 1) * hz):
            arrived(tt.at[rows(far * blk_rows + q * zrows, zrows)], ttf_recv.at[q])

    near(0)
    cross_term(1, 0)
    core_stage(1, 0)
    cross_term(2, 0)
    core_stage(2, 0)
    ss = final(0, 0)
    ss = ss + final(0, 1)
    x_stage1(1, 0)
    x_stage1(2, 0)
    near(1)
    x_stage2(1, 0)
    x_stage2(2, 0)
    cross_term(1, 1)
    core_stage(1, 1)
    cross_term(2, 1)
    core_stage(2, 1)
    x_stage1(1, 1)
    x_stage1(2, 1)
    z_stage(1, 0)
    z_stage(2, 0)
    distant(0)
    cross_term(3, 0)
    core_stage(3, 0)
    x_direct(0)
    distant(1)
    cross_term(3, 1)
    core_stage(3, 1)
    x_stage2(1, 1)
    x_stage2(2, 1)
    x_direct(1)
    ss = ss + final(1, 0)
    ss = ss + final(2, 0)
    z_stage(3, 0)
    z_stage(1, 1)
    z_stage(2, 1)
    z_stage(3, 1)
    ss = ss + final(3, 0)
    ss = ss + final(1, 1)
    ss = ss + final(2, 1)
    ss = ss + final(3, 1)

    def add_slots(ref, n):
        total = ref[0]
        for k in range(1, n):
            total = total + ref[k]
        return total

    ssz[z] = ss
    for d in order[::-1][:-1]:
        send(ssz.at[z], ssz.at[z], ss_send.at[0], ss_recv.at[0], at_blk(zpeer(d) * nxc + xc))
    arrived(ssz.at[pl.ds(0, nz - 1)], ss_recv.at[0])
    slot = y * nxc + xc
    ssp[slot] = add_slots(ssz, nz)
    peers = list(plane_peers())
    for peer in peers[::-1]:
        send(ssp.at[slot], ssp.at[slot], ss_send.at[1], ss_recv.at[1], peer)
    arrived(ssp.at[pl.ds(0, len(peers))], ss_recv.at[1])
    total = jnp.sum(add_slots(ssp, NY * nxc), keepdims=True)
    size = no * no * NA * NY * NB * NY
    rms_ref[...] = jnp.sqrt(total / size)

    arrived(tb.at[rows(0, 2 * blk_rows)], ty_send)
    arrived(tb.at[rows(0, blk_rows)], tf_send)
    arrived(a1.at[rows(0, (nz - 1) * zrows)], z_send)
    arrived(tt.at[rows(0, nz * (nxc - 1) * ROWS)], c_send)
    arrived(tt.at[rows(0, 2 * blk_rows)], tty_send)
    arrived(tt.at[rows(0, blk_rows)], ttf_send)
    arrived(ra, ra_send)
    arrived(rx, rx_send)
    arrived(rb, rb_send)
    arrived(rd, rd_send)
    arrived(rc, rc_send)
    arrived(ssz.at[pl.ds(0, nz - 1)], ss_send.at[0])
    arrived(ssp.at[pl.ds(0, len(peers))], ss_send.at[1])


def contractions(nz, nx, *args):
    nxc = nx * 2
    no = nz * nxc
    n = NB * no
    np = 2 * NY
    pc = n // 2
    dma = pltpu.SemaphoreType.DMA
    return pl.pallas_call(
        functools.partial(kernel, nz, nx),
        out_shape=(jax.ShapeDtypeStruct((NY * NB, NA, no), F32), jax.ShapeDtypeStruct((1, 1), F32)),
        in_specs=[pl.BlockSpec(memory_space=pl.ANY)] * 6,
        out_specs=(pl.BlockSpec(memory_space=pltpu.VMEM), pl.BlockSpec(memory_space=pltpu.VMEM)),
        scratch_shapes=[
            pltpu.VMEM((NY * no * ROWS + ROWS, 128), F32),
            pltpu.VMEM((NY * no * ROWS + ROWS, 128), F32),
            pltpu.VMEM((no * ROWS, 128), F32),
            pltpu.VMEM(((NA + 1) * no * CT, 128), F32),
            pltpu.VMEM(((NA + 1) * no * CT, 128), F32),
            pltpu.VMEM((1, no), F32),
            pltpu.VMEM((1, NA * NY), F32),
            pltpu.VMEM((1, NB * NY), F32),
            pltpu.VMEM((np, NA, pc), F32),
            pltpu.VMEM((NA * no, 2 * KT), BF16),
            pltpu.VMEM((n, 2 * KT), BF16),
            pltpu.VMEM((NY, nz * nx, 2, NA, n), F32),
            pltpu.VMEM((np, nz * nx, NA, pc), F32),
            pltpu.VMEM((np, nz, nx, NA, pc), F32),
            pltpu.VMEM((np - 2, 2, nz // 2, NA, pc), F32),
            pltpu.VMEM((np - 2, 2, nz, NA, pc), F32),
            pltpu.VMEM((2, 3, nz, NA, pc), F32),
            pltpu.VMEM((np, nz, NA, pc), F32),
            pltpu.VMEM((np, nz - 1, NA, pc), F32),
            pltpu.VMEM((nz, 1, 128), F32),
            pltpu.VMEM((NY * nxc, 1, 128), F32),
            dma((6,)),
            dma, dma((2, 2)), dma, dma((2,)),
            dma, dma((nz,)), dma, dma((nz,)), dma((nz,)),
            dma, dma((2, nz)), dma, dma((nz,)),
            dma, dma((np,)), dma, dma((np - 2, 2)), dma, dma((np - 2, 2)), dma, dma((2,)),
            dma, dma((np,)),
            dma((2,)), dma((2,)),
        ],
        compiler_params=pltpu.CompilerParams(collective_id=0, has_side_effects=True),
    )(*args)


def per_device(nz, nx, amplitudes, cycle_integrals, cross_integrals, occ_energy, vir_energy_a, vir_energy_b):
    no = nz * nx * 2
    t = amplitudes.reshape(no, NB, CT, 128).transpose(0, 2, 1, 3).reshape(no * ROWS, 128)
    w = cycle_integrals.reshape(NA * no * CT, 128)
    x = cross_integrals.reshape(NA * no * CT, 128)
    update, rms = contractions(
        nz, nx, t, w, x, occ_energy.reshape(1, -1), vir_energy_a.reshape(1, -1), vir_energy_b.reshape(1, -1))
    return update.transpose(1, 0, 2)[None], rms.reshape(())


def solution(mesh, nz=8, nx=4):
    return jax.shard_map(
        functools.partial(per_device, nz, nx),
        mesh=mesh,
        in_specs=(
            P("blk", None, "rep", None),
            P("rep", None, "blk", None),
            P("rep", None, "blk", None),
            P(),
            P(),
            P(),
        ),
        out_specs=(P("blk", "rep", None, None), P()),
        check_vma=False,
    )
```

time: 83 us -> 79.3 us (0.955)
  local copies, waits for them, and re-layouts: 4.57 us -> 1.48 us
  between operations: 0.66 us -> 2.39 us
  other arithmetic: 1.43 us -> 0 us
    slice x1 -> x0, local copies, waits for them, and re-layouts: 1.19 us -> none  [per_device(): return (residual / denom, rms[0, 0])]
    reshape x1 -> x0, local copies, waits for them, and re-layouts: 0.84 us -> none  [per_device(): residual = res.reshape(1, NA, NB * NY, no)]
    pallas_call x1, Pallas kernels: 76.1 us -> 75.3 us  [contractions(): pl.pallas_call(functools.partial(kernel, nz, nx), out_shape=(jax.ShapeDty...]
    unnamed x6 -> x1, local copies, waits for them, and re-layouts: 1.89 us -> 1.48 us
where the time goes in v2:
time: 79.3 us; the launch traced here: 79.1 us
  Pallas kernels  75.3 us (95%)
  between operations  2.39 us (3%)
  local copies, waits for them, and re-layouts  1.48 us (2%)
    pallas_call x1, Pallas kernels, contractions(): pl.pallas_call(functools.partial(kernel, nz, nx), out_shape=(jax.ShapeDty...  75.3 us

profile of v2, /device:TPU:1, one launch (start us, length us, event | category | flops | bytes accessed | tf_op | source)
XLA Modules:
  0.0 79.1 jit_solution(837527936712619594)
XLA Ops:
  0.6 75.3 %shard_map.77 = (f32[16,8,64]{2,1,0:T(8,128)}, f32[1,1]{1,0:T(1,128)}) custom-call(f32[1024,128]{1,0:T(8,128)} %bitcast.16, f32[2048,128]{1,0:T(8,128)} %bitcast.14, f32[2048,128]{1,0:T(8,128)} %bitcast.15, f32[1,64]{1,0:T(1,128)} %bitcast.18, f32[1,32]{1,0:T(1,128)} %bitcast.19, f32[1,16]{1,0:T(1,128)} %bitcast.20), custom_call_target="tpu_custom_call" | custom-call | tf_op jit(solution)/shard_map/pallas_call | solution.py:416
  75.9 1.5 %copy.9 = f32[1,8,16,64]{3,2,1,0:T(8,128)} copy(f32[1,8,16,64]{3,1,2,0:T(8,128)} %bitcast.17) | data formatting | bytes 65536

commit v3 on v2

--- a/solution.py
+++ b/solution.py
@@ -315,8 +315,6 @@
     arrived(tb.at[rows(far * blk_rows, half)], tf_recv.at[0])
     arrived(tb.at[rows(far * blk_rows + half, half)], tf_recv.at[1])
     cycle_term(3)
-    z_stage(0, 0)
-    z_stage(0, 1)
 
     def near(h):
         for q in range(h * hz, (h + 1) * hz):
@@ -335,24 +333,24 @@
     core_stage(1, 0)
     cross_term(2, 0)
     core_stage(2, 0)
-    ss = final(0, 0)
-    ss = ss + final(0, 1)
+    z_stage(0, 0)
+    z_stage(0, 1)
     x_stage1(1, 0)
     x_stage1(2, 0)
     near(1)
-    x_stage2(1, 0)
-    x_stage2(2, 0)
     cross_term(1, 1)
     core_stage(1, 1)
     cross_term(2, 1)
     core_stage(2, 1)
+    x_stage2(1, 0)
+    x_stage2(2, 0)
     x_stage1(1, 1)
     x_stage1(2, 1)
-    z_stage(1, 0)
-    z_stage(2, 0)
     distant(0)
     cross_term(3, 0)
     core_stage(3, 0)
+    z_stage(1, 0)
+    z_stage(2, 0)
     x_direct(0)
     distant(1)
     cross_term(3, 1)
@@ -360,12 +358,14 @@
     x_stage2(1, 1)
     x_stage2(2, 1)
     x_direct(1)
-    ss = ss + final(1, 0)
-    ss = ss + final(2, 0)
     z_stage(3, 0)
     z_stage(1, 1)
     z_stage(2, 1)
     z_stage(3, 1)
+    ss = final(0, 0)
+    ss = ss + final(0, 1)
+    ss = ss + final(1, 0)
+    ss = ss + final(2, 0)
     ss = ss + final(3, 0)
     ss = ss + final(1, 1)
     ss = ss + final(2, 1)

time: 79.3 us -> 74.9 us (0.945)
  Pallas kernels: 75.3 us -> 70.9 us
    pallas_call x1, Pallas kernels: 75.3 us -> 70.9 us  [contractions(): pl.pallas_call(functools.partial(kernel, nz, nx), out_shape=(jax.ShapeDty...]
where the time goes in v3:
time: 74.9 us; the launch traced here: 74.7 us
  Pallas kernels  70.9 us (95%)
  between operations  2.39 us (3%)
  local copies, waits for them, and re-layouts  1.48 us (2%)
    pallas_call x1, Pallas kernels, contractions(): pl.pallas_call(functools.partial(kernel, nz, nx), out_shape=(jax.ShapeDty...  70.9 us

profile of v3, /device:TPU:1, one launch (start us, length us, event | category | flops | bytes accessed | tf_op | source)
XLA Modules:
  0.0 74.7 jit_solution(9958666942421813434)
XLA Ops:
  0.6 70.9 %shard_map.77 = (f32[16,8,64]{2,1,0:T(8,128)}, f32[1,1]{1,0:T(1,128)}) custom-call(f32[1024,128]{1,0:T(8,128)} %bitcast.16, f32[2048,128]{1,0:T(8,128)} %bitcast.14, f32[2048,128]{1,0:T(8,128)} %bitcast.15, f32[1,64]{1,0:T(1,128)} %bitcast.18, f32[1,32]{1,0:T(1,128)} %bitcast.19, f32[1,16]{1,0:T(1,128)} %bitcast.20), custom_call_target="tpu_custom_call" | custom-call | tf_op jit(solution)/shard_map/pallas_call | solution.py:416
  71.5 1.5 %copy.9 = f32[1,8,16,64]{3,2,1,0:T(8,128)} copy(f32[1,8,16,64]{3,1,2,0:T(8,128)} %bitcast.17) | data formatting | bytes 65536

commit v4 on v3

--- a/solution.py
+++ b/solution.py
@@ -31,10 +31,10 @@
 def kernel(
     nz, nx,
     t_hbm, w_hbm, x_hbm, occ_hbm, va_hbm, vb_hbm, upd_ref, rms_ref,
-    tb, tt, a1, wv, xv, occ_v, va_v, vb_v, den, wop, top, part, ra, s1, rx, rb, rd, s2, rc, ssz, ssp,
+    tb, tt, a1, a2, wv, xv, occ_v, va_v, vb_v, den, wop, top, part, ra, s1, rx, rb, rd, s2, rc, ssz, ssp,
     load_sem, ty_send, ty_recv, tf_send, tf_recv, z_send, z_recv, c_send, c_recv, c_loc,
     tty_send, tty_recv, ttf_send, ttf_recv, ra_send, ra_recv, rx_send, rx_recv, rb_send, rb_recv, rd_send, rd_recv, rc_send, rc_recv,
-    ss_send, ss_recv,
+    ss_send, ss_recv, e_send, e_recv, e_loc, g_send, g_recv, f_send, f_recv, f_loc,
 ):
     nxc = nx * 2
     no = nz * nxc
@@ -48,6 +48,7 @@
     right, left, across = (x + 1) % nx, (x + nx - 1) % nx, (x + 2) % nx
     slot_y = (y, down, up, far)
     order = ring_order(nz)
+    close = order[:3]
 
     def at_y(yy):
         return {"blk": me, "rep": yy}
@@ -105,16 +106,18 @@
         send(t_hbm.at[rows(zp * zrows, zrows)], a1.at[rows(z * zrows, zrows)],
              z_send, z_recv.at[z], at_blk(zp * nxc + xc))
 
-    def second_stage(src, zs):
+    def second_stage(src, base, yb, zs, ssem, rsem, lsem):
+        to = yb * blk_rows + zs * zrows + xc * ROWS
         for d in range(1, nxc):
             p = xcpeer(d)
-            send(src.at[rows(zs * zrows + p * ROWS, ROWS)], tt.at[rows(mine + zs * zrows + xc * ROWS, ROWS)],
-                 c_send, c_recv.at[zs], at_blk(z * nxc + p))
-        pltpu.make_async_copy(
-            src.at[rows(zs * zrows + xc * ROWS, ROWS)], tt.at[rows(mine + zs * zrows + xc * ROWS, ROWS)],
-            c_loc.at[zs]).start()
-
-    second_stage(t_hbm, z)
+            send(src.at[rows(base + p * ROWS, ROWS)], tt.at[rows(to, ROWS)], ssem, rsem, at_blk(z * nxc + p))
+        pltpu.make_async_copy(src.at[rows(base + xc * ROWS, ROWS)], tt.at[rows(to, ROWS)], lsem).start()
+
+    def second_arrived(yb, zs, rsem, lsem):
+        arrived(tt.at[rows(yb * blk_rows + zs * zrows, zrows - ROWS)], rsem)
+        arrived(tt.at[rows(yb * blk_rows + zs * zrows, ROWS)], lsem)
+
+    second_stage(t_hbm, z * zrows, y, z, c_send, c_recv.at[z], c_loc.at[z])
     load_w = pltpu.make_async_copy(w_hbm, wv.at[pl.ds(0, NA * no * CT)], load_sem.at[0])
     load_x = pltpu.make_async_copy(x_hbm, xv.at[pl.ds(0, NA * no * CT)], load_sem.at[1])
     load_t = pltpu.make_async_copy(t_hbm, tb.at[rows(mine, blk_rows)], load_sem.at[2])
@@ -273,7 +276,7 @@
     def relay_stage(d):
         zs = (z + d) % nz
         arrived(a1.at[rows(zs * zrows, zrows)], z_recv.at[zs])
-        second_stage(a1, zs)
+        second_stage(a1, zs * zrows, y, zs, c_send, c_recv.at[zs], c_loc.at[zs])
 
     load_w.wait()
     prep_integrals(wv, 0)
@@ -294,45 +297,86 @@
     cycle_term(0)
 
     for q in range(nz):
-        arrived(tt.at[rows(mine + q * zrows, zrows - ROWS)], c_recv.at[q])
-        arrived(tt.at[rows(mine + q * zrows, ROWS)], c_loc.at[q])
-        chunk = tt.at[rows(mine + q * zrows, zrows)]
-        send(chunk, chunk, tty_send, tty_recv.at[0, q], at_y(up))
-        send(chunk, chunk, tty_send, tty_recv.at[1, q], at_y(down))
-
+        second_arrived(y, q, c_recv.at[q], c_loc.at[q])
+
+        @pl.when(z != q)
+        def _():
+            chunk = tt.at[rows(mine + q * zrows, zrows)]
+            send(chunk, chunk, tty_send, tty_recv.at[0, q], at_y(up))
+            send(chunk, chunk, tty_send, tty_recv.at[1, q], at_y(down))
+
+    arrived(tb.at[rows(down * blk_rows + half, half)], ty_recv.at[0, 1])
+    second_stage(tb, down * blk_rows + z * zrows, down, z, e_send, e_recv.at[0], e_loc.at[0])
+    arrived(tb.at[rows(up * blk_rows, half)], ty_recv.at[1, 0])
+    second_stage(tb, up * blk_rows + z * zrows, up, z, e_send, e_recv.at[1], e_loc.at[1])
     cross_term(0, 0)
     core_stage(0, 0)
     cross_term(0, 1)
     core_stage(0, 1)
-    arrived(tb.at[rows(down * blk_rows + half, half)], ty_recv.at[0, 1])
+    arrived(tb.at[rows(far * blk_rows, half)], tf_recv.at[0])
+    arrived(tb.at[rows(far * blk_rows + half, half)], tf_recv.at[1])
+    for d in close[1:]:
+        zp = zpeer(d)
+        send(tb.at[rows(far * blk_rows + zp * zrows, zrows)], a2.at[rows(z * zrows, zrows)],
+             g_send, g_recv.at[z], at_blk(zp * nxc + xc))
+    second_stage(tb, far * blk_rows + z * zrows, far, z, f_send, f_recv.at[z], f_loc.at[z])
     cycle_term(1)
     x_stage1(0, 0)
     x_stage1(0, 1)
-    arrived(tb.at[rows(up * blk_rows, half)], ty_recv.at[1, 0])
     cycle_term(2)
     x_stage2(0, 0)
     x_stage2(0, 1)
-    arrived(tb.at[rows(far * blk_rows, half)], tf_recv.at[0])
-    arrived(tb.at[rows(far * blk_rows + half, half)], tf_recv.at[1])
     cycle_term(3)
+
+    def is_close(q):
+        apart = (q + nz - z) % nz
+        out = apart == close[0]
+        for d in close[1:]:
+            out = jnp.logical_or(out, apart == d)
+        return out
 
     def near(h):
         for q in range(h * hz, (h + 1) * hz):
-            for way, src_y in enumerate((down, up)):
+            @pl.when(z != q)
+            def _():
+                for way, src_y in enumerate((down, up)):
+                    arrived(tt.at[rows(src_y * blk_rows + q * zrows, zrows)], tty_recv.at[way, q])
+
+            @pl.when(jnp.logical_not(is_close(q)))
+            def _():
+                src_y, dst_y = ((down, up), (up, down))[q % 2]
                 chunk = tt.at[rows(src_y * blk_rows + q * zrows, zrows)]
-                arrived(chunk, tty_recv.at[way, q])
-                if q % 2 == way:
-                    send(chunk, chunk, ttf_send, ttf_recv.at[q], at_y((up, down)[way]))
+                send(chunk, chunk, ttf_send, ttf_recv.at[q], at_y(dst_y))
+
+            @pl.when(z == q)
+            def _():
+                second_arrived(down, q, e_recv.at[0], e_loc.at[0])
+                second_arrived(up, q, e_recv.at[1], e_loc.at[1])
+
+    def relay_far(d):
+        zs = (z + d) % nz
+        arrived(a2.at[rows(zs * zrows, zrows)], g_recv.at[zs])
+        second_stage(a2, zs * zrows, far, zs, f_send, f_recv.at[zs], f_loc.at[zs])
 
     def distant(h):
         for q in range(h * hz, (h + 1) * hz):
-            arrived(tt.at[rows(far * blk_rows + q * zrows, zrows)], ttf_recv.at[q])
+            @pl.when(is_close(q))
+            def _():
+                second_arrived(far, q, f_recv.at[q], f_loc.at[q])
+
+            @pl.when(jnp.logical_not(is_close(q)))
+            def _():
+                arrived(tt.at[rows(far * blk_rows + q * zrows, zrows)], ttf_recv.at[q])
 
     near(0)
+    for d in close[1:3]:
+        relay_far(d)
     cross_term(1, 0)
     core_stage(1, 0)
     cross_term(2, 0)
     core_stage(2, 0)
+    for d in close[3:]:
+        relay_far(d)
     z_stage(0, 0)
     z_stage(0, 1)
     x_stage1(1, 0)
@@ -395,8 +439,12 @@
     arrived(tb.at[rows(0, blk_rows)], tf_send)
     arrived(a1.at[rows(0, (nz - 1) * zrows)], z_send)
     arrived(tt.at[rows(0, nz * (nxc - 1) * ROWS)], c_send)
-    arrived(tt.at[rows(0, 2 * blk_rows)], tty_send)
-    arrived(tt.at[rows(0, blk_rows)], ttf_send)
+    arrived(tt.at[rows(0, 2 * (nz - 1) * zrows)], tty_send)
+    if nz > len(close):
+        arrived(tt.at[rows(0, (nz - len(close)) * zrows)], ttf_send)
+    arrived(tt.at[rows(0, 2 * (nxc - 1) * ROWS)], e_send)
+    arrived(tt.at[rows(0, len(close) * (nxc - 1) * ROWS)], f_send)
+    arrived(a2.at[rows(0, (len(close) - 1) * zrows)], g_send)
     arrived(ra, ra_send)
     arrived(rx, rx_send)
     arrived(rb, rb_send)
@@ -421,6 +469,7 @@
         scratch_shapes=[
             pltpu.VMEM((NY * no * ROWS + ROWS, 128), F32),
             pltpu.VMEM((NY * no * ROWS + ROWS, 128), F32),
+            pltpu.VMEM((no * ROWS, 128), F32),
             pltpu.VMEM((no * ROWS, 128), F32),
             pltpu.VMEM(((NA + 1) * no * CT, 128), F32),
             pltpu.VMEM(((NA + 1) * no * CT, 128), F32),
@@ -447,6 +496,7 @@
             dma, dma((np,)), dma, dma((np - 2, 2)), dma, dma((np - 2, 2)), dma, dma((2,)),
             dma, dma((np,)),
             dma((2,)), dma((2,)),
+            dma, dma((2,)), dma((2,)), dma, dma((nz,)), dma, dma((nz,)), dma((nz,)),
         ],
         compiler_params=pltpu.CompilerParams(collective_id=0, has_side_effects=True),
     )(*args)

time: 74.9 us -> 74 us (0.988)
  Pallas kernels: 70.9 us -> 69.9 us
    pallas_call x1, Pallas kernels: 70.9 us -> 69.9 us  [contractions(): pl.pallas_call(functools.partial(kernel, nz, nx), out_shape=(jax.ShapeDty...]
where the time goes in v4:
time: 74 us; the launch traced here: 73.8 us
  Pallas kernels  69.9 us (94%)
  between operations  2.39 us (3%)
  local copies, waits for them, and re-layouts  1.48 us (2%)
    pallas_call x1, Pallas kernels, contractions(): pl.pallas_call(functools.partial(kernel, nz, nx), out_shape=(jax.ShapeDty...  69.9 us
    unnamed x1, local copies, waits for them, and re-layouts  1.48 us

profile of v4, /device:TPU:1, one launch (start us, length us, event | category | flops | bytes accessed | tf_op | source)
XLA Modules:
  0.0 73.8 jit_solution(15397638252083888761)
XLA Ops:
  0.6 69.9 %shard_map.77 = (f32[16,8,64]{2,1,0:T(8,128)}, f32[1,1]{1,0:T(1,128)}) custom-call(f32[1024,128]{1,0:T(8,128)} %bitcast.16, f32[2048,128]{1,0:T(8,128)} %bitcast.14, f32[2048,128]{1,0:T(8,128)} %bitcast.15, f32[1,64]{1,0:T(1,128)} %bitcast.18, f32[1,32]{1,0:T(1,128)} %bitcast.19, f32[1,16]{1,0:T(1,128)} %bitcast.20), custom_call_target="tpu_custom_call" | custom-call | tf_op jit(solution)/shard_map/pallas_call | solution.py:464
  70.6 1.5 %copy.9 = f32[1,8,16,64]{3,2,1,0:T(8,128)} copy(f32[1,8,16,64]{3,1,2,0:T(8,128)} %bitcast.17) | data formatting | bytes 65536

commit v5 on v4

--- a/solution.py
+++ b/solution.py
@@ -396,11 +396,11 @@
     z_stage(1, 0)
     z_stage(2, 0)
     x_direct(0)
+    x_stage2(1, 1)
+    x_stage2(2, 1)
     distant(1)
     cross_term(3, 1)
     core_stage(3, 1)
-    x_stage2(1, 1)
-    x_stage2(2, 1)
     x_direct(1)
     z_stage(3, 0)
     z_stage(1, 1)

time: 74 us -> 73.9 us (level)
  no operation moved by 1% of the time
where the time goes in v5:
time: 73.9 us; the launch traced here: 73.7 us
  Pallas kernels  69.8 us (94%)
  between operations  2.39 us (3%)
  local copies, waits for them, and re-layouts  1.48 us (2%)
    pallas_call x1, Pallas kernels, contractions(): pl.pallas_call(functools.partial(kernel, nz, nx), out_shape=(jax.ShapeDty...  69.8 us
    unnamed x1, local copies, waits for them, and re-layouts  1.48 us

profile of v5, /device:TPU:1, one launch (start us, length us, event | category | flops | bytes accessed | tf_op | source)
XLA Modules:
  0.0 73.7 jit_solution(16675828448295895127)
XLA Ops:
  0.6 69.8 %shard_map.77 = (f32[16,8,64]{2,1,0:T(8,128)}, f32[1,1]{1,0:T(1,128)}) custom-call(f32[1024,128]{1,0:T(8,128)} %bitcast.16, f32[2048,128]{1,0:T(8,128)} %bitcast.14, f32[2048,128]{1,0:T(8,128)} %bitcast.15, f32[1,64]{1,0:T(1,128)} %bitcast.18, f32[1,32]{1,0:T(1,128)} %bitcast.19, f32[1,16]{1,0:T(1,128)} %bitcast.20), custom_call_target="tpu_custom_call" | custom-call | tf_op jit(solution)/shard_map/pallas_call | solution.py:464
  70.5 1.5 %copy.9 = f32[1,8,16,64]{3,2,1,0:T(8,128)} copy(f32[1,8,16,64]{3,1,2,0:T(8,128)} %bitcast.17) | data formatting | bytes 65536
